TPU v7x, 512 devices: a whole 4x8x8 slice. The times are simulated.
512 devices in a mesh: section: 2 (over z_lo), batch: 16 (over z_hi, x), tensor: 16 (over y, core).
Axes of the slice: x: 4, y: 8, z: 8 (z_hi: 4, z_lo: 2; z = z_hi * 2 + z_lo), core: 2. Of those that a mesh axis runs over, the one named last changes fastest.
Arguments:
- tokens: bfloat16 [4096, 4096], P('batch', ('section', 'tensor')), may hold values from -950 to 950, as said below
- nb_ids: int32 [128, 128], P('batch'), may hold values from 0 to 15999
- nb_index: int32 [64, 2], P('batch'), may hold values from 0 to 7
- table: bfloat16 [16000, 4096], P('batch', ('section', 'tensor')), may hold values from -950 to 950, as said below
- norm_gains: float32 [2, 4096], replicated, may hold values from 0.1 to 1.9
- projections: bfloat16 [2, 2, 4096, 4096], P(None, None, None, ('section', 'tensor')), may hold values from -0.5 to 0.5
Outputs:
- mixed: bfloat16 [4096, 4096], P('batch', ('section', 'tensor'))
Inputs may be any that keep to these rules, and one draw needn't show every extreme that they name: tokens: entries of order one to some hundreds, of both signs. table: entries of order one to some hundreds, of both signs.
All inputs are finite; a program needn't handle non-finite values.
Results may differ from a plain program's by a relative error of at most 0.019.
Values may be sent and summed in bfloat16 or wider, within the bound.
No kernel may reach another device: no remote copies, remote signals or barrier semaphores. Data moves between devices by JAX's collectives and lax.ppermute only.
A program may use at most 64 MiB of HBM per device.

v0:
```python
import math
import jax
import jax.numpy as jnp
from jax import lax
from jax.sharding import PartitionSpec as P

HEAD_DIM = 128
SPAN = 64
NEIGH = 2


def rms_norm(values, gain):
    wide = values.astype(jnp.float32)
    square = jnp.mean(wide * wide, axis=-1, keepdims=True)
    return (wide * lax.rsqrt(square + 1e-06) * gain).astype(jnp.bfloat16)


def on_device(tokens, nb_ids, nb_index, table, norm_gains, projections):
    piece_cols = table.shape[1]
    block_count, neighbour_len = nb_ids.shape
    nb_rows = block_count * neighbour_len
    flat_ids = nb_ids.reshape(nb_rows)
    piece = lax.all_gather(table, "batch", axis=0, tiled=True)
    inside = (flat_ids >= 0) & (flat_ids < piece.shape[0])
    picked = jnp.take(piece, jnp.clip(flat_ids, 0, piece.shape[0] - 1), axis=0)
    embedded = jnp.where(inside[:, None], picked, jnp.zeros((nb_rows, piece_cols), jnp.bfloat16))
    full_neighbours = lax.all_gather(embedded, ("section", "tensor"), axis=1, tiled=True)
    encoded = rms_norm(full_neighbours, norm_gains[0])
    key_value = jnp.einsum(
        "md,jdc->jmc", encoded, projections[0], preferred_element_type=jnp.float32
    ).astype(jnp.bfloat16)
    full_tokens = lax.all_gather(tokens, ("section", "tensor"), axis=1, tiled=True)
    normed = rms_norm(full_tokens, norm_gains[1])
    queries = jnp.dot(normed, projections[1, 0], preferred_element_type=jnp.float32).astype(
        jnp.bfloat16
    )
    tok_rows, head_cols = queries.shape
    local_heads = head_cols // HEAD_DIM
    span_count = tok_rows // SPAN
    query_blocks = queries.reshape(span_count, SPAN, local_heads, HEAD_DIM)
    stacked = key_value.reshape(2, block_count, neighbour_len, local_heads, HEAD_DIM)
    chosen = stacked[:, nb_index].reshape(
        2, span_count, NEIGH * neighbour_len, local_heads, HEAD_DIM
    )
    scores = jnp.einsum(
        "cqhd,ckhd->chqk", query_blocks, chosen[0], preferred_element_type=jnp.float32
    ) * (1.0 / math.sqrt(HEAD_DIM))
    expo = jnp.exp(scores)
    weights = (expo / jnp.sum(expo, axis=-1, keepdims=True)).astype(jnp.bfloat16)
    attended = jnp.einsum("chqk,ckhd->cqhd", weights, chosen[1], preferred_element_type=jnp.float32)
    attended = attended.astype(jnp.bfloat16).reshape(tok_rows, head_cols)
    out_weight = projections[1, 1]
    width = out_weight.shape[0]
    tensor_count = lax.axis_size("tensor")
    out_cols = width // (2 * tensor_count)
    grid = out_weight.reshape(2, tensor_count, out_cols, head_cols)
    partial_sums = jnp.einsum(
        "rh,stch->rtsc", attended, grid, preferred_element_type=jnp.float32
    ).reshape(tok_rows, width)
    within = lax.psum_scatter(
        partial_sums.astype(jnp.bfloat16), "tensor", scatter_dimension=1, tiled=True
    )
    result = lax.psum_scatter(within, "section", scatter_dimension=1, tiled=True).astype(
        jnp.float32
    )
    return result.astype(jnp.bfloat16)


def solution(mesh):
    return jax.shard_map(
        on_device,
        mesh=mesh,
        in_specs=(
            P("batch", ("section", "tensor")),
            P("batch", None),
            P("batch", None),
            P("batch", ("section", "tensor")),
            P(),
            P(None, None, None, ("section", "tensor")),
        ),
        out_specs=P("batch", ("section", "tensor")),
        check_vma=False,
    )
```

profile of v0, /device:TPU:1, one launch (start us, length us, event | category | flops | bytes accessed | tf_op | source)
XLA Modules:
  0.0 360.7 jit_solution(11192853730899416732)
XLA Ops:
  6.5 0.7 all-gather.4.cloned.1.call-update
  7.3 0.0 all-gather.8.cloned.1.call-start
  7.3 0.7 all-gather.8.cloned.1.call-update
  8.0 0.0 all-gather.6.cloned.1.call-start
  8.1 0.7 and_bitcast_fusion
  8.7 0.7 compare_and_fusion
  9.4 0.7 broadcast_clamp_fusion.1
  10.2 87.7 %all-gather.4.cloned.1.call-done = bf16[16000,128]{1,0:T(8,128)(2,1)} async-done(((bf16[1000,128]{1,0:T(8,128)(2,1)}), bf16[16000,128]{1,0:T(8,128)(2,1)}) %all-gather.4.cloned.1.call-update) | async-done | bytes 4096016 | tf_op jit(solution)/shard_map/all_gather | solution.py:23
  97.9 5.6 %gather_fusion = bf16[1024,128]{1,0:T(8,128)(2,1)S(1)} fusion(bf16[16000,128]{1,0:T(8,128)(2,1)} %all-gather.4.cloned.1.call-done, s32[1024]{0:T(1024)S(1)} %broadcast_clamp_fusion), kind=kCustom, calls=%fused_computation | custom fusion | bytes 528384 | tf_op jit(solution)/shard_map/jit(_take)/gather | solution.py:25
  103.4 1.0 select_select_fusion
  104.5 0.0 all-gather.6.cloned.1.call-update
  104.5 0.0 reduce-scatter.3.cloned.1.call-start
  104.6 0.7 compare_select_fusion.2
  105.2 0.1 copy.9
  105.3 0.1 reshape.120
  105.4 1.3 slice.29
  106.8 61.8 %all-gather.8.cloned.1.call-done = bf16[256,4096]{1,0:T(8,128)(2,1)} async-done(((bf16[256,128]{1,0:T(8,128)(2,1)}), bf16[256,4096]{1,0:T(8,128)(2,1)}) %all-gather.8.cloned.1.call-update) | async-done | bytes 2097168 | tf_op jit(solution)/shard_map/all_gather | solution.py:32
  168.5 2.1 fusion.6
  170.6 2.7 fusion.21
  173.3 85.6 %all-gather.6.cloned.1.call-done = bf16[1024,4096]{1,0:T(8,128)(2,1)} async-done(((bf16[1024,128]{1,0:T(8,128)(2,1)}), bf16[1024,4096]{1,0:T(8,128)(2,1)}) %all-gather.6.cloned.1.call-update) | async-done | bytes 8388624 | tf_op jit(solution)/shard_map/all_gather | solution.py:27
  258.9 5.2 %fusion = f32[1024]{0:T(1024)S(1)} fusion(bf16[1024,4096]{1,0:T(8,128)(2,1)} %all-gather.6.cloned.1.call-done), kind=kLoop, calls=%fused_computation.4 | loop fusion | flops 12581888 | bytes 8392704 | tf_op jit(solution)/shard_map/reduce_sum | solution.py:14
  264.2 0.5 copy-done
  264.7 4.0 %fusion.15 = bf16[1024,2,128]{2,0,1:T(8,128)(2,1)S(1)} fusion(bf16[2,2,4096,128]{3,2,1,0:T(8,128)(2,1)} %param.11, bf16[1024,4096]{1,0:T(8,128)(2,1)S(1)} %copy-done, f32[4096]{0:T(1024)S(1)} %bitcast.63, f32[1024]{0:T(1024)S(1)} %add_rsqrt_fusion), kind=kOutput, calls=%fused_computation.20 | convolution fusion | flops 2164523008 | bytes 11030528 | tf_op jit(solution)/shard_map/md,jdc->jmc/dot_general | solution.py:29
  268.8 0.6 gather_fusion.1
  269.5 0.2 fusion.20
  269.7 0.2 convolution_convert_fusion
  270.0 0.7 convert_bitcast_fusion
  270.7 1.5 copy.11
  272.2 0.0 reduce-scatter.5.cloned.1.call-start
  272.2 58.8 %reduce-scatter.3.cloned.1.call-done = bf16[256,256]{0,1:T(8,128)(2,1)} async-done(((bf16[256,4096]{0,1:T(8,128)(2,1)}), bf16[256,256]{0,1:T(8,128)(2,1)}) %reduce-scatter.3.cloned.1.call-update) | async-done | bytes 131088 | tf_op jit(solution)/shard_map/reduce_scatter | solution.py:60
  331.1 21.5 %reduce-scatter.5.cloned.1.call-done = bf16[256,128]{0,1:T(8,128)(2,1)} async-done(((bf16[256,256]{0,1:T(8,128)(2,1)}), bf16[256,128]{0,1:T(8,128)(2,1)}) %reduce-scatter.5.cloned.1.call-update) | async-done | bytes 65552 | tf_op jit(solution)/shard_map/reduce_scatter | solution.py:63
  352.6 1.6 copy.12
  (14 shorter events, 0.2 us)
Async XLA Ops:
  6.5 100.2 %copy-start.1 = (f32[2,4096]{1,0:T(2,128)S(1)}, f32[2,4096]{1,0:T(2,128)}, u32[]{:S(2)}) copy-start(f32[2,4096]{1,0:T(2,128)} %param.10) | copy-start | bytes 98308
  6.5 91.3 %all-gather.4.cloned.1.call-start = ((), (), s32[]{:S(2)}) async-start(), calls=%async_computation.2 | async-start | bytes 4352000 | tf_op jit(solution)/shard_map/all_gather | solution.py:23
  7.3 161.3 %all-gather.8.cloned.1.call-start = ((), (), s32[]{:S(2)}) async-start(), calls=%async_computation.4 | async-start | bytes 2162688 | tf_op jit(solution)/shard_map/all_gather | solution.py:32
  8.0 250.9 %all-gather.6.cloned.1.call-start = ((), (), s32[]{:S(2)}) async-start(), calls=%async_computation.3 | async-start | bytes 8650752 | tf_op jit(solution)/shard_map/all_gather | solution.py:27
  104.5 226.5 %reduce-scatter.3.cloned.1.call-start = ((), (), s32[]{:S(2)}) async-start(), calls=%async_computation.5 | async-start | bytes 2228224 | tf_op jit(solution)/shard_map/reduce_scatter | solution.py:60
  258.9 5.8 %copy-start = (bf16[1024,4096]{1,0:T(8,128)(2,1)S(1)}, bf16[1024,4096]{1,0:T(8,128)(2,1)}, u32[]{:S(2)}) copy-start(bf16[1024,4096]{1,0:T(8,128)(2,1)} %all-gather.6.cloned.1.call-done) | copy-start | bytes 25165828
  272.2 80.4 %reduce-scatter.5.cloned.1.call-start = ((), (), s32[]{:S(2)}) async-start(), calls=%async_computation.6 | async-start | bytes 196608 | tf_op jit(solution)/shard_map/reduce_scatter | solution.py:63
Sparse Core Ops, SparseCore 0:
  10.4 87.4 all-gather.3
  99.9 68.5 all-gather.7
  170.6 88.2 all-gather.5
  272.3 58.6 reduce-scatter.2
  333.6 18.8 reduce-scatter.4
where the time goes:
time: 361 us
  waiting for transfers between devices  317 us (88%)
  between operations  13.2 us (4%)
  local copies, waits for them, and re-layouts  11.4 us (3%)
  other arithmetic  11.1 us (3%)
  matrix products  7.87 us (2%)
    all_gather x1, waiting for transfers between devices, on_device(): piece = lax.all_gather(table, 'batch', axis=0, tiled=True)  87.7 us
    all_gather x1, waiting for transfers between devices, on_device(): lax.all_gather(embedded, ('section', 'tensor'), axis=1, tiled=True)  85.6 us
    all_gather x1, waiting for transfers between devices, on_device(): lax.all_gather(tokens, ('section', 'tensor'), axis=1, tiled=True)  61.8 us
    reduce_scatter x1, waiting for transfers between devices, on_device(): lax.psum_scatter(partial_sums.astype(jnp.bfloat16), 'tensor', scatter_dim...  58.8 us
    reduce_scatter x1, waiting for transfers between devices, on_device(): lax.psum_scatter(within, 'section', scatter_dimension=1, tiled=True)  21.5 us
    reduce_sum x2, other arithmetic, rms_norm(): square = jnp.mean(wide * wide, axis=-1, keepdims=True)  7.3 us
  transfers between devices with their start and end apart: 5, of which 5 were waited for; matrix products, arithmetic and copies ran while one was open for 4% of the time, Pallas kernels for 0%

commit v1 on v0

--- a/solution.py
+++ b/solution.py
@@ -7,6 +7,15 @@
 HEAD_DIM = 128
 SPAN = 64
 NEIGH = 2
+
+
+def convert_the_sites(content, peer_axis):
+    steps_seen = []
+    for _ in range(lax.axis_size(peer_axis)):
+        steps_seen.append(content)
+    far_arr = jnp.stack(steps_seen, axis=0)
+    odd = lax.all_to_all(far_arr, peer_axis, 0, 0)
+    return jnp.concatenate(odd, axis=1)
 
 
 def rms_norm(values, gain):
@@ -29,7 +38,7 @@
     key_value = jnp.einsum(
         "md,jdc->jmc", encoded, projections[0], preferred_element_type=jnp.float32
     ).astype(jnp.bfloat16)
-    full_tokens = lax.all_gather(tokens, ("section", "tensor"), axis=1, tiled=True)
+    full_tokens = convert_the_sites(tokens, ("section", "tensor"))
     normed = rms_norm(full_tokens, norm_gains[1])
     queries = jnp.dot(normed, projections[1, 0], preferred_element_type=jnp.float32).astype(
         jnp.bfloat16

time: 361 us -> 330 us (0.914)
  waiting for transfers between devices: 317 us -> 277 us
  starting transfers between devices: 0.16 us -> 8.93 us
    all_gather x1 -> x0, waiting for transfers between devices: 61.8 us -> none  [on_device(): lax.all_gather(tokens, ('section', 'tensor'), axis=1, tiled=True)]
    all_to_all x0 -> x1, waiting for transfers between devices: none -> 60 us  [convert_the_sites(): odd = lax.all_to_all(far_arr, peer_axis, 0, 0)]
    all_gather x1, waiting for transfers between devices: 85.6 us -> 49.3 us  [on_device(): lax.all_gather(embedded, ('section', 'tensor'), axis=1, tiled=True)]
    all_to_all x0 -> x1, starting transfers between devices: none -> 8.8 us  [convert_the_sites(): odd = lax.all_to_all(far_arr, peer_axis, 0, 0)]
  transfers between devices with their start and end apart: 5 -> 5, of which waited for: 5 -> 5; matrix products, arithmetic and copies ran while one was open for 4% -> 3% of each run, Pallas kernels for 0% -> 0%
where the time goes in v1:
time: 330 us
  waiting for transfers between devices  277 us (84%)
  local copies, waits for them, and re-layouts  13.9 us (4%)
  between operations  13.3 us (4%)
  other arithmetic  9.68 us (3%)
  starting transfers between devices  8.93 us (3%)
  matrix products  7.2 us (2%)
    all_gather x1, waiting for transfers between devices, on_device(): piece = lax.all_gather(table, 'batch', axis=0, tiled=True)  88.5 us
    all_to_all x1, waiting for transfers between devices, convert_the_sites(): odd = lax.all_to_all(far_arr, peer_axis, 0, 0)  60 us
    reduce_scatter x1, waiting for transfers between devices, on_device(): lax.psum_scatter(partial_sums.astype(jnp.bfloat16), 'tensor', scatter_dim...  56.8 us
    all_gather x1, waiting for transfers between devices, on_device(): lax.all_gather(embedded, ('section', 'tensor'), axis=1, tiled=True)  49.3 us
    reduce_scatter x1, waiting for transfers between devices, on_device(): lax.psum_scatter(within, 'section', scatter_dimension=1, tiled=True)  21.5 us
    all_to_all x1, starting transfers between devices, convert_the_sites(): odd = lax.all_to_all(far_arr, peer_axis, 0, 0)  8.8 us
  transfers between devices with their start and end apart: 5, of which 5 were waited for; matrix products, arithmetic and copies ran while one was open for 3% of the time, Pallas kernels for 0%

profile of v1, /device:TPU:1, one launch (start us, length us, event | category | flops | bytes accessed | tf_op | source)
XLA Modules:
  0.0 329.8 jit_solution(16381598644253557920)
XLA Ops:
  6.5 0.7 all-gather.3.cloned.1.call-update
  7.3 0.0 all-gather.5.cloned.1.call-start
  7.3 0.7 and_bitcast_fusion
  8.0 0.7 compare_and_fusion
  8.7 0.7 broadcast_clamp_fusion.1
  9.4 88.5 %all-gather.3.cloned.1.call-done = bf16[16000,128]{1,0:T(8,128)(2,1)} async-done(((bf16[1000,128]{1,0:T(8,128)(2,1)}), bf16[16000,128]{1,0:T(8,128)(2,1)}) %all-gather.3.cloned.1.call-update) | async-done | bytes 4096016 | tf_op jit(solution)/shard_map/all_gather | solution.py:32
  97.9 5.6 %gather_fusion = bf16[1024,128]{1,0:T(8,128)(2,1)S(1)} fusion(bf16[16000,128]{1,0:T(8,128)(2,1)} %all-gather.3.cloned.1.call-done, s32[1024]{0:T(1024)S(1)} %broadcast_clamp_fusion), kind=kCustom, calls=%fused_computation | custom fusion | bytes 528384 | tf_op jit(solution)/shard_map/jit(_take)/gather | solution.py:34
  103.4 1.0 select_select_fusion
  104.5 0.9 copy.11
  105.5 1.6 stack.2
  107.1 8.8 %all-to-all-start = ((bf16[32,256,128]{1,2,0:T(8,128)(2,1)}), bf16[32,256,128]{1,2,0:T(8,128)(2,1)S(1)}, u32[]{:S(2)}, u32[]{:S(2)}) async-start(bf16[32,256,128]{1,2,0:T(8,128)(2,1)} %stack.2), calls=%async_computation | async-start | bytes 4194304 | tf_op jit(solution)/shard_map/all_to_all | solution.py:17
  115.9 0.0 reduce-scatter.3.cloned.1.call-start
  115.9 0.1 copy.9
  116.0 0.1 reshape.135
  116.1 1.3 slice.29
  117.5 60.0 %all-to-all-done = bf16[32,256,128]{1,2,0:T(8,128)(2,1)S(1)} async-done(((bf16[32,256,128]{1,2,0:T(8,128)(2,1)}), bf16[32,256,128]{1,2,0:T(8,128)(2,1)S(1)}, u32[]{:S(2)}, u32[]{:S(2)}) %all-to-all-start) | async-done | bytes 2097184 | tf_op jit(solution)/shard_map/all_to_all | solution.py:17
  177.4 0.6 fusion.6
  178.0 0.7 fusion.8
  178.8 2.0 convolution_convert_fusion
  180.8 49.3 %all-gather.5.cloned.1.call-done = bf16[1024,4096]{1,0:T(8,128)(2,1)} async-done(((bf16[1024,128]{1,0:T(8,128)(2,1)}), bf16[1024,4096]{1,0:T(8,128)(2,1)}) %all-gather.5.cloned.1.call-update) | async-done | bytes 8388624 | tf_op jit(solution)/shard_map/all_gather | solution.py:36
  230.0 5.2 %fusion = f32[1024]{0:T(1024)S(1)} fusion(bf16[1024,4096]{1,0:T(8,128)(2,1)} %all-gather.5.cloned.1.call-done), kind=kLoop, calls=%fused_computation.4 | loop fusion | flops 12581888 | bytes 8392704 | tf_op jit(solution)/shard_map/reduce_sum | solution.py:23
  235.3 0.5 copy-done
  235.8 4.0 %fusion.11 = bf16[1024,2,128]{2,0,1:T(8,128)(2,1)S(1)} fusion(bf16[2,2,4096,128]{3,2,1,0:T(8,128)(2,1)} %param.11, bf16[1024,4096]{1,0:T(8,128)(2,1)S(1)} %copy-done, f32[4096]{0:T(1024)S(1)} %bitcast.69, f32[1024]{0:T(1024)S(1)} %add_rsqrt_fusion), kind=kOutput, calls=%fused_computation.17 | convolution fusion | flops 2164523008 | bytes 11030528 | tf_op jit(solution)/shard_map/md,jdc->jmc/dot_general | solution.py:38
  239.9 0.6 gather_fusion.1
  240.6 0.2 fusion.16
  240.8 0.2 convolution_convert_fusion.1
  241.1 0.7 convert_bitcast_fusion
  241.8 1.5 copy.12
  243.3 0.0 reduce-scatter.5.cloned.1.call-start
  243.3 56.8 %reduce-scatter.3.cloned.1.call-done = bf16[256,256]{0,1:T(8,128)(2,1)} async-done(((bf16[256,4096]{0,1:T(8,128)(2,1)}), bf16[256,256]{0,1:T(8,128)(2,1)}) %reduce-scatter.3.cloned.1.call-update) | async-done | bytes 131088 | tf_op jit(solution)/shard_map/reduce_scatter | solution.py:69
  300.2 21.5 %reduce-scatter.5.cloned.1.call-done = bf16[256,128]{0,1:T(8,128)(2,1)} async-done(((bf16[256,256]{0,1:T(8,128)(2,1)}), bf16[256,128]{0,1:T(8,128)(2,1)}) %reduce-scatter.5.cloned.1.call-update) | async-done | bytes 65552 | tf_op jit(solution)/shard_map/reduce_scatter | solution.py:72
  321.7 1.6 copy.13
  (18 shorter events, 0.2 us)
Async XLA Ops:
  6.5 91.3 %all-gather.3.cloned.1.call-start = ((), (), s32[]{:S(2)}) async-start(), calls=%async_computation.3 | async-start | bytes 4352000 | tf_op jit(solution)/shard_map/all_gather | solution.py:32
  7.3 222.8 %all-gather.5.cloned.1.call-start = ((), (), s32[]{:S(2)}) async-start(), calls=%async_computation.4 | async-start | bytes 8650752 | tf_op jit(solution)/shard_map/all_gather | solution.py:36
  103.4 12.5 %copy-start.2 = (s32[4,2]{0,1:T(2,128)S(1)}, s32[4,2]{0,1:T(2,128)}, u32[]{:S(2)}) copy-start(s32[4,2]{0,1:T(2,128)} %param.8) | copy-start | bytes 100
  105.5 12.0 %copy-start.1 = (f32[2,4096]{1,0:T(2,128)S(1)}, f32[2,4096]{1,0:T(2,128)}, u32[]{:S(2)}) copy-start(f32[2,4096]{1,0:T(2,128)} %param.10) | copy-start | bytes 98308
  107.1 70.4 %all-to-all-start = ((bf16[32,256,128]{1,2,0:T(8,128)(2,1)}), bf16[32,256,128]{1,2,0:T(8,128)(2,1)S(1)}, u32[]{:S(2)}, u32[]{:S(2)}) async-start(bf16[32,256,128]{1,2,0:T(8,128)(2,1)} %stack.2), calls=%async_computation | async-start | bytes 4194304 | tf_op jit(solution)/shard_map/all_to_all | solution.py:17
  115.9 184.3 %reduce-scatter.3.cloned.1.call-start = ((), (), s32[]{:S(2)}) async-start(), calls=%async_computation.5 | async-start | bytes 2228224 | tf_op jit(solution)/shard_map/reduce_scatter | solution.py:69
  230.0 5.8 %copy-start = (bf16[1024,4096]{1,0:T(8,128)(2,1)S(1)}, bf16[1024,4096]{1,0:T(8,128)(2,1)}, u32[]{:S(2)}) copy-start(bf16[1024,4096]{1,0:T(8,128)(2,1)} %all-gather.5.cloned.1.call-done) | copy-start | bytes 25165828
  243.3 78.4 %reduce-scatter.5.cloned.1.call-start = ((), (), s32[]{:S(2)}) async-start(), calls=%async_computation.6 | async-start | bytes 196608 | tf_op jit(solution)/shard_map/reduce_scatter | solution.py:72
Sparse Core Ops, SparseCore 0:
  10.4 87.4 all-gather.2
  104.6 125.3 all-gather.4
  243.4 56.6 reduce-scatter.2
  302.7 18.8 reduce-scatter.4
